TPU v7x, 32 devices: a whole 2x2x4 slice. The times are simulated.
32 devices in a mesh: dp: 8 (over y, x, core), seq: 4 (over z).
Axes of the slice: x: 2, y: 2, z: 4, core: 2. Of those that a mesh axis runs over, the one named last changes fastest.
Arguments:
- queries: bfloat16 [8, 4, 512, 32, 128], P('dp', 'seq'), may hold values from -6 to 6
- key_rows: bfloat16 [8, 4, 512, 32, 128], P('dp', 'seq'), may hold values from -6 to 6
- value_rows: bfloat16 [8, 4, 512, 32, 128], P('dp', 'seq'), may hold values from -6 to 6
- destination: int32 [8, 4, 512], P('dp', 'seq'), may hold values from 0 to 7, as said below
- doc_starts: int32 [8, 4, 512], P('dp', 'seq'), may hold values 0 or 1
- decay_rate: float32 [32], replicated, may hold values from 7.6293945e-06 to 0.04
- norm_gain: float32 [32, 128], replicated, may hold values from 0.1 to 1.9
Outputs:
- attended: bfloat16 [8, 4, 512, 32, 128], P('dp', 'seq')
Inputs may be any that keep to these rules, and one draw needn't show every extreme that they name: `destination`: each loader sends at most 96 of its rows to one sequence; at each seq index one sequence, drawn afresh, receives exactly 96 rows from every loader.
All inputs are finite; a program needn't handle non-finite values. No bound on the sum of `doc_starts` on one device may be relied on, other than what follows from the above.
Results may differ from a plain program's by a relative error of at most 0.0055.
Values may be sent and summed in bfloat16 or wider, within the bound.
A program may use at most 192 MiB of HBM per device.

v0:
```python
import functools
import jax
import jax.numpy as jnp
from jax import lax
from jax.experimental import pallas as pl
from jax.experimental.pallas import tpu as pltpu
from jax.sharding import PartitionSpec as P

MESH = pl.DeviceIdType.MESH
F32 = jnp.float32
BF16 = jnp.bfloat16
eps_norm = 1e-06
HG = 8
HO = 16
HC = 2
ZT = jnp.float32
ZLAG = 4


def update_kernel(seqs, cap, flat_ref, k_ref, v_ref, q_ref, kw_ref, u_ref, ko, vo, qo, hot, tall, wide):
    d = u_ref.shape[-1]
    rows = k_ref.shape[0]

    @pl.when(pl.program_id(0) == 0)
    def _():
        place = lax.broadcasted_iota(jnp.int32, hot.shape, 0)
        hot[...] = jnp.where(place == flat_ref[...], 1.0, 0.0).astype(BF16)

    for x_ref, o_ref in ((k_ref, ko), (v_ref, vo), (q_ref, qo)):
        tall[...] = x_ref[...].astype(F32).reshape(rows * HG, d)
        for j in range(HG):
            wide[:, j * d : (j + 1) * d] = tall[pl.ds(j, rows, stride=HG), :].astype(BF16)
        for j in range(HG // 2):
            cols = slice(2 * j * d, 2 * (j + 1) * d)
            moved = jnp.dot(hot[...], wide[:, cols], preferred_element_type=F32)
            o_ref[:, cols] = moved.astype(BF16)

    def body(g, _):
        here = pl.ds(pl.multiple_of(g * cap, 16), cap)
        weight = kw_ref[0, here, :]
        for j in range(HG):
            cols = slice(j * d, (j + 1) * d)
            scaled = (ko[here, cols].astype(F32) * weight[:, j : j + 1]).astype(BF16)
            update = lax.dot_general(
                scaled, vo[here, cols], (((0,), (0,)), ((), ())), preferred_element_type=F32
            )
            u_ref[pl.ds(g, 1), j] = update.astype(BF16)[None]
        return 0

    lax.fori_loop(0, seqs, body, 0)


def updates_of(flat, key, value, query, key_weight, seqs, cap):
    rows, heads, d = key.shape
    total = seqs * cap
    kw = key_weight.reshape(total, heads // HG, HG).transpose(1, 0, 2)
    natural = pl.BlockSpec((rows, HG, d), lambda i: (0, i, 0))
    packed = pl.BlockSpec((total, HG * d), lambda i: (0, i))
    packed_shape = jax.ShapeDtypeStruct((total, heads * d), BF16)
    return pl.pallas_call(
        functools.partial(update_kernel, seqs, cap),
        grid=(heads // HG,),
        out_shape=[jax.ShapeDtypeStruct((seqs, heads, d, d), BF16)] + [packed_shape] * 3,
        in_specs=[
            pl.BlockSpec((1, rows), lambda i: (0, 0)),
            natural,
            natural,
            natural,
            pl.BlockSpec((1, total, HG), lambda i: (i, 0, 0)),
        ],
        out_specs=[pl.BlockSpec((seqs, HG, d, d), lambda i: (0, i, 0, 0)), packed, packed, packed],
        scratch_shapes=[
            pltpu.VMEM((total, rows), BF16),
            pltpu.VMEM((rows * HG, d), F32),
            pltpu.VMEM((rows, HG * d), BF16),
        ],
        compiler_params=pltpu.CompilerParams(vmem_limit_bytes=56 * 1024 * 1024),
    )(flat.reshape(1, rows), key, value, query, kw)


def scan_kernel(levels, shards, seqs, heads, *refs):
    fact_ref, rate_ref, u_ref, out_ref = refs[:4]
    cur = [u_ref] + list(refs[4 : 4 + levels - 1])
    facts, dec, f_s, f_r = refs[3 + levels : 7 + levels]
    refs = refs[7 + levels :]
    got = refs[:levels]
    put = refs[levels : 2 * levels]
    total, zin = refs[2 * levels : 2 * levels + 2]
    up_s, up_r, dn_s, dn_r, z_s, z_r = refs[2 * levels + 2 :]
    me = lax.axis_index("dp")
    shard = lax.axis_index("seq")
    chunks = heads // HC

    def bit(k):
        return lax.rem(lax.div(me, 2**k), 2)

    def partner(k):
        return me + 2**k - bit(k) * (2 ** (k + 1))

    def low(k):
        return lax.rem(me, 2**k)

    def decay(table, seq, head):
        return dec[table * seqs + seq, pl.ds(head, 1), :]

    barrier = pltpu.get_barrier_semaphore()
    for i in range(1, seqs):
        peer = lax.rem(me + i, seqs)
        pl.semaphore_signal(barrier, inc=1, device_id=(peer, shard), device_id_type=MESH)

    @pl.when(shard > 0)
    def _():
        pl.semaphore_signal(barrier, inc=1, device_id=(me, shard - 1), device_id_type=MESH)

    @pl.when(shard < shards - 1)
    def _():
        pl.semaphore_signal(barrier, inc=1, device_id=(me, shard + 1), device_id_type=MESH)

    ends = (shard > 0).astype(jnp.int32) + (shard < shards - 1).astype(jnp.int32)
    pl.semaphore_wait(barrier, seqs - 1 + ends)

    @pl.when(shard == 0)
    def _():
        def clear(i, _):
            zin[pl.ds(i, 1)] = jnp.zeros((1,) + zin.shape[1:], zin.dtype)
            return 0

        lax.fori_loop(0, heads, clear, 0)

    def part(c):
        return pl.ds(c * HC, HC)

    def up_copy(k, c):
        return pltpu.make_async_remote_copy(
            src_ref=cur[k].at[:, 1 - bit(k), part(c)],
            dst_ref=got[k].at[:, part(c)],
            send_sem=up_s.at[k, c],
            recv_sem=up_r.at[k, c],
            device_id=(partner(k), shard),
            device_id_type=MESH,
        )

    def down_copy(k, c, j, receive):
        owner = partner(k) if receive else me
        seq = j * 2 ** (k + 1) + lax.rem(owner, 2 ** (k + 1))
        slot = 2 ** (levels - k - 1) - 1 + j
        return pltpu.make_async_remote_copy(
            src_ref=put[k].at[j, part(c)],
            dst_ref=out_ref.at[seq, part(c)],
            send_sem=dn_s.at[slot, c],
            recv_sem=dn_r.at[slot, c],
            device_id=(partner(k), shard),
            device_id_type=MESH,
        )

    def z_copy(c, target):
        return pltpu.make_async_remote_copy(
            src_ref=total.at[part(c)],
            dst_ref=zin.at[part(c)],
            send_sem=z_s.at[c],
            recv_sem=z_r.at[c],
            device_id=(me, target),
            device_id_type=MESH,
        )

    def up(k, c):
        up_copy(k, c).wait_recv()
        mine = bit(k)
        first = (mine == 0).astype(F32)
        share = 2 ** (levels - k - 1)

        def body(i, _):
            j, head = lax.div(i, HC), c * HC + lax.rem(i, HC)
            seq = j * 2 ** (k + 1) + low(k + 1)
            own = cur[k][j, mine, head].astype(F32)
            other = got[k][j, head].astype(F32)
            hi = decay(k, seq, head)
            own_w = first * hi + (1.0 - first)
            other_w = first + (1.0 - first) * hi
            both = own * own_w + other * other_w
            if k + 1 < levels:
                cur[k + 1][lax.div(j, 2), lax.rem(j, 2), head] = both.astype(BF16)
            else:
                total[head] = both.astype(total.dtype)
            return 0

        lax.fori_loop(0, share * HC, body, 0)
        if k + 1 < levels:
            up_copy(k + 1, c).start()

    def across(c):
        @pl.when(shard > 0)
        def _():
            z_copy(c, shard).wait_recv()

        def body(i, _):
            head = c * HC + i
            state = zin[head]
            out_ref[me, head] = state.astype(BF16)
            nxt = state.astype(F32) * decay(2 * levels, me, head) + total[head].astype(F32)
            total[head] = nxt.astype(total.dtype)
            return 0

        lax.fori_loop(0, HC, body, 0)

        @pl.when(shard < shards - 1)
        def _():
            z_copy(c, shard + 1).start()

    def down(k, c):
        if k + 1 < levels:
            for j in range(2 ** (levels - k - 2)):
                down_copy(k + 1, c, j, True).wait_recv()
        mine = bit(k)
        first = (mine == 0).astype(F32)
        share = 2 ** (levels - k - 1)

        def body(i, _):
            j, head = lax.div(i, HC), c * HC + lax.rem(i, HC)
            seq = j * 2 ** (k + 1) + low(k + 1)
            base = out_ref[seq, head].astype(F32)
            own = cur[k][j, mine, head].astype(F32)
            other = got[k][j, head].astype(F32)
            lo = first * own + (1.0 - first) * other
            later = base * decay(levels + k, seq, head) + lo
            out_ref[seq, head] = (first * base + (1.0 - first) * later).astype(BF16)
            put[k][j, head] = (first * later + (1.0 - first) * base).astype(BF16)
            return 0

        lax.fori_loop(0, share * HC, body, 0)
        for j in range(share):
            down_copy(k, c, j, False).start()

    def fact_copy(i):
        return pltpu.make_async_remote_copy(
            src_ref=fact_ref,
            dst_ref=facts.at[me],
            send_sem=f_s.at[i - 1],
            recv_sem=f_r.at[i - 1],
            device_id=(lax.rem(me + i, seqs), shard),
            device_id_type=MESH,
        )

    def fact_arrival(i):
        return pltpu.make_async_remote_copy(
            src_ref=fact_ref,
            dst_ref=facts.at[lax.rem(me + seqs - i, seqs)],
            send_sem=f_s.at[i - 1],
            recv_sem=f_r.at[i - 1],
            device_id=(lax.rem(me + i, seqs), shard),
            device_id_type=MESH,
        )

    for i in range(1, seqs):
        fact_copy(i).start()
    for c in range(chunks):
        up_copy(0, c).start()
    facts[pl.ds(me, 1)] = fact_ref[...][None]
    for i in range(1, seqs):
        fact_arrival(i).wait_recv()
    rate = rate_ref[...]
    spans = [((me // 2 ** (k + 1) * 2 + 1) * 2**k, 2**k) for k in range(levels)]
    spans += [((me // 2 ** (k + 1) * 2) * 2**k, 2**k) for k in range(levels)]
    spans += [(me * 0, seqs)]
    for table, (begin, size) in enumerate(spans):
        count = jnp.zeros(fact_ref.shape[1:], F32)
        docs = jnp.zeros(fact_ref.shape[1:], F32)
        for loader in range(seqs):
            inside = ((loader >= begin) & (loader < begin + size)).astype(F32)
            count = count + facts[loader, 0] * inside
            docs = docs + facts[loader, 1] * inside
        for seq in range(seqs):
            gone = jnp.exp(-rate * count[seq : seq + 1])
            dec[table * seqs + seq] = jnp.where(docs[seq : seq + 1] == 0.0, gone, 0.0)
    z_lag = levels - 1 + ZLAG
    for t in range(chunks + z_lag + levels + 1):
        for k in range(levels):
            if 0 <= t - k < chunks:
                up(k, t - k)
        if 0 <= t - z_lag < chunks:
            across(t - z_lag)
        for k in range(levels - 1, -1, -1):
            c = t - z_lag - (levels - 1 - k)
            if 0 <= c < chunks:
                down(k, c)
    for c in range(chunks):
        for j in range(2 ** (levels - 1)):
            down_copy(0, c, j, True).wait_recv()
        for k in range(levels):
            up_copy(k, c).wait_send()
            for j in range(2 ** (levels - k - 1)):
                down_copy(k, c, j, False).wait_send()

    for i in range(1, seqs):
        fact_copy(i).wait_send()

    @pl.when(shard < shards - 1)
    def _():
        for c in range(chunks):
            z_copy(c, shard + 1).wait_send()


def scan_states(facts, rate, updates, levels, shards, call):
    seqs, heads, d = updates.shape[:3]
    chunks = heads // HC
    vm = pltpu.VMEM
    share = [2 ** (levels - k - 1) for k in range(levels)]
    dma = pltpu.SemaphoreType.DMA
    return pl.pallas_call(
        functools.partial(scan_kernel, levels, shards, seqs, heads),
        out_shape=jax.ShapeDtypeStruct((seqs, heads, d, d), BF16),
        in_specs=[
            pl.BlockSpec(memory_space=pltpu.VMEM),
            pl.BlockSpec(memory_space=pltpu.VMEM),
            pl.BlockSpec(memory_space=pltpu.VMEM),
        ],
        out_specs=pl.BlockSpec(memory_space=pltpu.VMEM),
        scratch_shapes=[vm((share[k], 2, heads, d, d), BF16) for k in range(1, levels)]
        + [vm((seqs,) + facts.shape, F32), vm(((2 * levels + 1) * seqs, heads, d), F32)]
        + [dma((seqs - 1,)), dma((seqs - 1,))]
        + [vm((share[k], heads, d, d), BF16) for k in range(levels)]
        + [vm((share[k], heads, d, d), BF16) for k in range(levels)]
        + [vm((heads, d, d), ZT), vm((heads, d, d), ZT)]
        + [dma((levels, chunks)), dma((levels, chunks))]
        + [dma((seqs - 1, chunks)), dma((seqs - 1, chunks))]
        + [dma((chunks,)), dma((chunks,))],
        compiler_params=pltpu.CompilerParams(
            collective_id=call, has_side_effects=True, vmem_limit_bytes=60 * 1024 * 1024
        ),
    )(facts, rate, updates.reshape(seqs // 2, 2, heads, d, d))


def finish_kernel(
    heads, d, rate_ref, flat_ref, q_ref, k_ref, v_ref, state_ref, col_ref, row_ref, cw_ref, gain_ref,
    o_ref, mixed, normed, tall
):
    cap = q_ref.shape[0]
    g = pl.program_id(0)
    ri = lax.broadcasted_iota(jnp.int32, (cap, cap), 0)
    ci = lax.broadcasted_iota(jnp.int32, (cap, cap), 1)
    keep = (ri >= ci) & (col_ref[...] == row_ref[0])
    gap = jnp.maximum(ri - ci, 0).astype(F32)
    carry = cw_ref[...]
    squares = jnp.zeros((cap, d), F32)
    for h in range(heads):
        cols = slice(h * d, (h + 1) * d)
        q = q_ref[:, cols]
        scores = lax.dot_general(
            q, k_ref[:, cols], (((1,), (1,)), ((), ())), preferred_element_type=F32
        )
        weight = jnp.where(keep, jnp.exp(-rate_ref[h] * gap), 0.0)
        half = (scores * weight).astype(BF16)
        intra = jnp.dot(half, v_ref[:, cols], preferred_element_type=F32)
        inter = jnp.dot(q, state_ref[0, h], preferred_element_type=F32)
        out = intra + inter * carry[:, h : h + 1]
        mixed[:, cols] = out
        squares = squares + out * out
    mean = jnp.sum(squares, axis=1, keepdims=True) * (1.0 / (heads * d))
    scale = lax.rsqrt(mean + eps_norm)
    for h in range(heads):
        cols = slice(h * d, (h + 1) * d)
        result = (mixed[:, cols] * scale * gain_ref[:, cols]).astype(BF16)
        normed[pl.ds(pl.multiple_of(g * cap, 16), cap), cols] = result

    @pl.when(g == pl.num_programs(0) - 1)
    def _():
        rows, total = o_ref.shape[0], normed.shape[0]
        place = lax.broadcasted_iota(jnp.int32, (rows, total), 1)
        hot = jnp.where(place == flat_ref[...], 1.0, 0.0).astype(BF16)
        for i in range(heads // HO):
            for j in range(0, HO, 2):
                h = i * HO + j
                back = jnp.dot(hot, normed[:, h * d : (h + 2) * d], preferred_element_type=F32)
                tall[pl.ds(j, rows, stride=HO), :] = back[:, :d]
                tall[pl.ds(j + 1, rows, stride=HO), :] = back[:, d:]
            o_ref[:, i * HO : (i + 1) * HO, :] = tall[...].reshape(rows, HO, d).astype(BF16)


def finish(rate, flat, query, key, value, states, doc, carry_weight, gain, seqs, cap, heads, d):
    total = seqs * cap
    rows = flat.shape[0]
    wide = pl.BlockSpec((cap, heads * d), lambda g: (g, 0))
    return pl.pallas_call(
        functools.partial(finish_kernel, heads, d),
        grid=(seqs,),
        out_shape=jax.ShapeDtypeStruct((rows, heads, d), BF16),
        in_specs=[
            pl.BlockSpec(memory_space=pltpu.SMEM),
            pl.BlockSpec((rows, 1), lambda g: (0, 0)),
            wide,
            wide,
            wide,
            pl.BlockSpec((1, heads, d, d), lambda g: (g, 0, 0, 0)),
            pl.BlockSpec((cap, 1), lambda g: (g, 0)),
            pl.BlockSpec((1, 1, cap), lambda g: (g, 0, 0)),
            pl.BlockSpec((cap, heads), lambda g: (g, 0)),
            pl.BlockSpec((1, heads * d), lambda g: (0, 0)),
        ],
        out_specs=pl.BlockSpec((rows, heads, d), lambda g: (0, 0, 0)),
        scratch_shapes=[
            pltpu.VMEM((cap, heads * d), F32),
            pltpu.VMEM((total, heads * d), BF16),
            pltpu.VMEM((rows * HO, d), F32),
        ],
        compiler_params=pltpu.CompilerParams(vmem_limit_bytes=56 * 1024 * 1024),
    )(
        rate,
        flat.reshape(rows, 1),
        query,
        key,
        value,
        states,
        doc.reshape(total, 1),
        doc.reshape(seqs, 1, cap),
        carry_weight,
        gain.reshape(1, heads * d),
    )


def per_device(queries, key_rows, value_rows, destination, doc_starts, decay_rate, norm_gain):
    loaders = lax.axis_size("dp")
    shards = lax.axis_size("seq")
    rows, heads, d = queries.shape[2:]
    cap = 3 * rows // (2 * loaders)
    levels = loaders.bit_length() - 1
    total = loaders * cap
    dest = destination[0, 0]
    start = doc_starts[0, 0]
    r = jnp.arange(rows, dtype=jnp.int32)
    earlier = (dest[:, None] == dest[None, :]) & (r[None, :] < r[:, None])
    slot = jnp.sum(earlier.astype(jnp.int32), axis=1)
    flat = dest * cap + slot
    place = jnp.arange(total, dtype=jnp.int32)
    hit = place[:, None] == flat[None, :]
    begin = jnp.sum(jnp.where(hit, start[None, :], 0), axis=1).reshape(loaders, cap)
    targets = jnp.arange(loaders, dtype=jnp.int32)
    number = jnp.sum((dest[None, :] == targets[:, None]).astype(jnp.int32), axis=1)
    position = jnp.arange(cap, dtype=jnp.int32)
    upto = (position[None, :] <= position[:, None]).astype(jnp.int32)
    doc = jnp.sum(begin[:, None, :] * upto[None], axis=2)
    doc_end = jnp.sum(begin, axis=1)

    facts = jnp.broadcast_to(jnp.stack([number, doc_end]).astype(F32)[:, :, None], (2, loaders, d))
    rate = jnp.broadcast_to(decay_rate[:, None], (heads, d))

    until = jnp.maximum(number[:, None] - 1 - position[None, :], 0).astype(F32)
    key_keep = (position[None, :] < number[:, None]) & (doc == doc_end[:, None])
    key_weight = jnp.where(
        key_keep[:, :, None], jnp.exp(-decay_rate[None, None, :] * until[:, :, None]), 0.0
    ).reshape(total, heads)
    since = (position + 1).astype(F32)
    carry_weight = jnp.where(
        (doc == 0)[:, :, None], jnp.exp(-decay_rate[None, None, :] * since[None, :, None]), 0.0
    ).reshape(total, heads)

    updates, key, value, query = updates_of(
        flat, key_rows[0, 0], value_rows[0, 0], queries[0, 0], key_weight, loaders, cap
    )
    passes = max(1, loaders // 8)
    width = heads // passes
    states = [
        scan_states(
            facts,
            rate[i * width : (i + 1) * width],
            updates[:, i * width : (i + 1) * width],
            levels,
            shards,
            i,
        )
        for i in range(passes)
    ]
    states = states[0] if passes == 1 else jnp.concatenate(states, axis=1)
    attended = finish(
        decay_rate, flat, query, key, value, states, doc, carry_weight, norm_gain, loaders, cap, heads, d
    )
    return attended[None, None]


def solution(mesh):
    placed = (
        P("dp", "seq", None, None, None),
        P("dp", "seq", None, None, None),
        P("dp", "seq", None, None, None),
        P("dp", "seq", None),
        P("dp", "seq", None),
        P(),
        P(),
    )
    return jax.shard_map(
        per_device,
        mesh=mesh,
        in_specs=placed,
        out_specs=P("dp", "seq", None, None, None),
        check_vma=False,
    )
```

profile of v0, /device:TPU:27, one launch (start us, length us, event | category | flops | bytes accessed | tf_op | source)
XLA Modules:
  0.0 207.1 jit_solution(9606039292747446127)
XLA Ops:
  0.0 0.0 copy-start
  0.0 1.0 convert_reduce_fusion
  1.0 0.7 multiply_add_fusion
  1.7 0.9 select_reduce_fusion
  2.6 0.1 mul.87
  2.7 0.2 multiply_reduce_fusion
  2.9 0.0 copy-start.1
  3.0 0.1 reduce_sum.55
  3.1 0.8 convert_reduce_fusion.1
  3.9 0.1 broadcast_compare_fusion
  3.9 0.1 and.15
  4.0 0.1 maximum_convert_fusion
  4.1 0.1 convert_element_type.41
  4.2 0.7 neg.5
  4.9 0.1 mul.91
  4.9 1.4 exponential_select_fusion.kw_ref
  6.4 0.0 copy-done
  6.4 0.6 bitcast_add_fusion.flat_ref
  7.0 0.0 copy-start.2
  7.0 34.0 %shard_map.73 = (bf16[8,32,128,128]{3,2,1,0:T(8,128)(2,1)}, bf16[768,4096]{1,0:T(8,128)(2,1)}, bf16[768,4096]{1,0:T(8,128)(2,1)}, bf16[768,4096]{1,0:T(8,128)(2,1)}) custom-call(s32[1,512]{1,0:T(1,128)} %bitcast_add_fusion.flat_ref, bf16[512,32,128]{2,1,0:T(8,128)(2,1)} %bitcast.20, bf16[512,32,128]{2,1,0:T(8,128)(2,1)} %bitcast.21, ...), custom_call_target="tpu_custom_call" | custom-call | tf_op jit(solution)/shard_map/pallas_call | solution.py:60
  41.0 0.7 broadcast_in_dim.87.refs_0_
  41.7 0.0 copy-done.2
  41.7 0.7 broadcast_in_dim.88.refs_1_
  42.4 127.1 %shard_map.74.state_ref = bf16[8,32,128,128]{3,2,1,0:T(8,128)(2,1)} custom-call(f32[2,8,128]{2,1,0:T(8,128)} %broadcast_in_dim.87.refs_0_, f32[32,128]{1,0:T(8,128)} %broadcast_in_dim.88.refs_1_, bf16[4,2,32,128,128]{4,3,2,1,0:T(8,128)(2,1)} %bitcast.19), custom_call_target="tpu_custom_call" | custom-call | tf_op jit(solution)/shard_map/pallas_call | solution.py:309
  169.5 0.1 eq.77
  169.6 0.1 multiply_exponential_fusion
  169.7 1.0 bitcast_select_fusion.cw_ref
  170.6 0.0 copy-done.1
  170.6 1.1 reshape.216.col_ref
  171.7 0.9 copy.17.flat_ref
  172.6 34.5 %shard_map.75 = bf16[512,32,128]{2,1,0:T(8,128)(2,1)} custom-call(f32[32]{0:T(128)} %rate_ref.1, s32[512,1]{1,0:T(8,128)} %copy.17.flat_ref, bf16[768,4096]{1,0:T(8,128)(2,1)} %get-tuple-element.9.q_ref, bf16[768,4096]{1,0:T(8,128)(2,1)} %get-tuple-element.10.k_ref, bf16[768,4096]{1,0:T(8,128)(2,1)} %get-tuple-element.11.v_ref, ...), custom_call_target="tpu_custom_call" | custom-call | tf_op jit(solution)/shard_map/pallas_call | solution.py:383
  (5 shorter events, 0.0 us)
Async XLA Ops:
  0.0 6.4 %copy-start = (s32[1,1,512]{2,1,0:T(1,128)S(1)}, s32[1,1,512]{2,1,0:T(1,128)}, u32[]{:S(2)}) copy-start(s32[1,1,512]{2,1,0:T(1,128)} %param.10) | copy-start | bytes 6148
  2.9 167.7 %copy-start.1 = (s32[8,96]{1,0:T(8,128)}, s32[8,96]{1,0:T(8,128)S(1)}, u32[]{:S(2)}) copy-start(s32[8,96]{1,0:T(8,128)S(1)} %multiply_reduce_fusion) | copy-start | bytes 9220
  7.0 34.7 %copy-start.2 = (f32[32]{0:T(128)S(1)}, f32[32]{0:T(128)}, u32[]{:S(2)}) copy-start(f32[32]{0:T(128)} %rate_ref.1) | copy-start | bytes 388
where the time goes:
time: 207 us
  Pallas kernels  196 us (95%)
  other arithmetic  7.66 us (4%)
  local copies, waits for them, and re-layouts  3.7 us (2%)
    pallas_call x1, Pallas kernels, scan_states(): pl.pallas_call(functools.partial(scan_kernel, levels, shards, seqs, heads...  127 us
    pallas_call x1, Pallas kernels, finish(): pl.pallas_call(functools.partial(finish_kernel, heads, d), grid=(seqs,),...  34.5 us
    pallas_call x1, Pallas kernels, updates_of(): pl.pallas_call(functools.partial(update_kernel, seqs, cap), grid=(heads /...  34 us

commit v1 on v0

--- a/solution.py
+++ b/solution.py
@@ -17,76 +17,20 @@
 ZLAG = 4
 
 
-def update_kernel(seqs, cap, flat_ref, k_ref, v_ref, q_ref, kw_ref, u_ref, ko, vo, qo, hot, tall, wide):
-    d = u_ref.shape[-1]
-    rows = k_ref.shape[0]
-
-    @pl.when(pl.program_id(0) == 0)
-    def _():
-        place = lax.broadcasted_iota(jnp.int32, hot.shape, 0)
-        hot[...] = jnp.where(place == flat_ref[...], 1.0, 0.0).astype(BF16)
-
-    for x_ref, o_ref in ((k_ref, ko), (v_ref, vo), (q_ref, qo)):
-        tall[...] = x_ref[...].astype(F32).reshape(rows * HG, d)
-        for j in range(HG):
-            wide[:, j * d : (j + 1) * d] = tall[pl.ds(j, rows, stride=HG), :].astype(BF16)
-        for j in range(HG // 2):
-            cols = slice(2 * j * d, 2 * (j + 1) * d)
-            moved = jnp.dot(hot[...], wide[:, cols], preferred_element_type=F32)
-            o_ref[:, cols] = moved.astype(BF16)
-
-    def body(g, _):
-        here = pl.ds(pl.multiple_of(g * cap, 16), cap)
-        weight = kw_ref[0, here, :]
-        for j in range(HG):
-            cols = slice(j * d, (j + 1) * d)
-            scaled = (ko[here, cols].astype(F32) * weight[:, j : j + 1]).astype(BF16)
-            update = lax.dot_general(
-                scaled, vo[here, cols], (((0,), (0,)), ((), ())), preferred_element_type=F32
-            )
-            u_ref[pl.ds(g, 1), j] = update.astype(BF16)[None]
-        return 0
-
-    lax.fori_loop(0, seqs, body, 0)
-
-
-def updates_of(flat, key, value, query, key_weight, seqs, cap):
-    rows, heads, d = key.shape
-    total = seqs * cap
-    kw = key_weight.reshape(total, heads // HG, HG).transpose(1, 0, 2)
-    natural = pl.BlockSpec((rows, HG, d), lambda i: (0, i, 0))
-    packed = pl.BlockSpec((total, HG * d), lambda i: (0, i))
-    packed_shape = jax.ShapeDtypeStruct((total, heads * d), BF16)
-    return pl.pallas_call(
-        functools.partial(update_kernel, seqs, cap),
-        grid=(heads // HG,),
-        out_shape=[jax.ShapeDtypeStruct((seqs, heads, d, d), BF16)] + [packed_shape] * 3,
-        in_specs=[
-            pl.BlockSpec((1, rows), lambda i: (0, 0)),
-            natural,
-            natural,
-            natural,
-            pl.BlockSpec((1, total, HG), lambda i: (i, 0, 0)),
-        ],
-        out_specs=[pl.BlockSpec((seqs, HG, d, d), lambda i: (0, i, 0, 0)), packed, packed, packed],
-        scratch_shapes=[
-            pltpu.VMEM((total, rows), BF16),
-            pltpu.VMEM((rows * HG, d), F32),
-            pltpu.VMEM((rows, HG * d), BF16),
-        ],
-        compiler_params=pltpu.CompilerParams(vmem_limit_bytes=56 * 1024 * 1024),
-    )(flat.reshape(1, rows), key, value, query, kw)
-
-
-def scan_kernel(levels, shards, seqs, heads, *refs):
-    fact_ref, rate_ref, u_ref, out_ref = refs[:4]
-    cur = [u_ref] + list(refs[4 : 4 + levels - 1])
-    facts, dec, f_s, f_r = refs[3 + levels : 7 + levels]
-    refs = refs[7 + levels :]
+def scan_kernel(levels, shards, seqs, heads, cap, *refs):
+    fact_ref, rate_ref, flat_ref, k_ref, v_ref, q_ref, kw_ref, out_ref = refs[:8]
+    packed = refs[8:11]
+    refs = refs[11:]
+    u_ref, hot, tall, wide, moved, pack_sem = refs[:6]
+    refs = refs[6:]
+    cur = [u_ref] + list(refs[: levels - 1])
+    facts, dec, f_s, f_r = refs[levels - 1 : 3 + levels]
+    refs = refs[3 + levels :]
     got = refs[:levels]
-    put = refs[levels : 2 * levels]
-    total, zin = refs[2 * levels : 2 * levels + 2]
-    up_s, up_r, dn_s, dn_r, z_s, z_r = refs[2 * levels + 2 :]
+    put = got
+    total, zin = refs[levels : levels + 2]
+    up_s, up_r, dn_s, dn_r, z_s, z_r = refs[levels + 2 :]
+    rows, _, d = k_ref.shape
     me = lax.axis_index("dp")
     shard = lax.axis_index("seq")
     chunks = heads // HC
@@ -253,8 +197,47 @@
 
     for i in range(1, seqs):
         fact_copy(i).start()
-    for c in range(chunks):
-        up_copy(0, c).start()
+    place = lax.broadcasted_iota(jnp.int32, hot.shape, 0)
+    hot[...] = jnp.where(place == flat_ref[...], 1.0, 0.0).astype(BF16)
+
+    def pack_copy(n, i):
+        return pltpu.make_async_copy(
+            moved.at[n], packed[n].at[:, pl.ds(i * HG * d, HG * d)], pack_sem.at[n]
+        )
+
+    def group(i):
+        for n, x_ref in enumerate((k_ref, v_ref, q_ref)):
+            if i > 0:
+                pack_copy(n, i - 1).wait()
+            tall[...] = x_ref[:, i * HG : (i + 1) * HG, :].astype(F32).reshape(rows * HG, d)
+            for j in range(HG):
+                wide[:, j * d : (j + 1) * d] = tall[pl.ds(j, rows, stride=HG), :].astype(BF16)
+            for j in range(HG // 2):
+                cols = slice(2 * j * d, 2 * (j + 1) * d)
+                rowsout = jnp.dot(hot[...], wide[:, cols], preferred_element_type=F32)
+                moved[n, :, cols] = rowsout.astype(BF16)
+            pack_copy(n, i).start()
+
+        def body(g, _):
+            here = pl.ds(pl.multiple_of(g * cap, 16), cap)
+            weight = kw_ref[i, here, :]
+            for j in range(HG):
+                cols = slice(j * d, (j + 1) * d)
+                scaled = (moved[0, here, cols].astype(F32) * weight[:, j : j + 1]).astype(BF16)
+                update = lax.dot_general(
+                    scaled,
+                    moved[1, here, cols],
+                    (((0,), (0,)), ((), ())),
+                    preferred_element_type=F32,
+                )
+                u_ref[lax.div(g, 2), lax.rem(g, 2), i * HG + j] = update.astype(BF16)
+            return 0
+
+        lax.fori_loop(0, seqs, body, 0)
+        for c in range(i * HG // HC, (i + 1) * HG // HC):
+            up_copy(0, c).start()
+
+    group(0)
     facts[pl.ds(me, 1)] = fact_ref[...][None]
     for i in range(1, seqs):
         fact_arrival(i).wait_recv()
@@ -273,7 +256,10 @@
             gone = jnp.exp(-rate * count[seq : seq + 1])
             dec[table * seqs + seq] = jnp.where(docs[seq : seq + 1] == 0.0, gone, 0.0)
     z_lag = levels - 1 + ZLAG
+    per_group = HG // HC
     for t in range(chunks + z_lag + levels + 1):
+        if t > 0 and t % per_group == 0 and t // per_group < heads // HG:
+            group(t // per_group)
         for k in range(levels):
             if 0 <= t - k < chunks:
                 up(k, t - k)
@@ -283,6 +269,8 @@
             c = t - z_lag - (levels - 1 - k)
             if 0 <= c < chunks:
                 down(k, c)
+    for n in range(3):
+        pack_copy(n, heads // HG - 1).wait()
     for c in range(chunks):
         for j in range(2 ** (levels - 1)):
             down_copy(0, c, j, True).wait_recv()
@@ -300,34 +288,41 @@
             z_copy(c, shard + 1).wait_send()
 
 
-def scan_states(facts, rate, updates, levels, shards, call):
-    seqs, heads, d = updates.shape[:3]
+def scan_states(facts, rate, flat, key, value, query, key_weight, levels, shards, cap, call):
+    rows, heads, d = key.shape
+    seqs = facts.shape[1]
+    total = seqs * cap
     chunks = heads // HC
     vm = pltpu.VMEM
     share = [2 ** (levels - k - 1) for k in range(levels)]
     dma = pltpu.SemaphoreType.DMA
+    kw = key_weight.reshape(total, heads // HG, HG).transpose(1, 0, 2)
+    packed_shape = jax.ShapeDtypeStruct((total, heads * d), BF16)
     return pl.pallas_call(
-        functools.partial(scan_kernel, levels, shards, seqs, heads),
-        out_shape=jax.ShapeDtypeStruct((seqs, heads, d, d), BF16),
-        in_specs=[
-            pl.BlockSpec(memory_space=pltpu.VMEM),
-            pl.BlockSpec(memory_space=pltpu.VMEM),
-            pl.BlockSpec(memory_space=pltpu.VMEM),
-        ],
-        out_specs=pl.BlockSpec(memory_space=pltpu.VMEM),
-        scratch_shapes=[vm((share[k], 2, heads, d, d), BF16) for k in range(1, levels)]
+        functools.partial(scan_kernel, levels, shards, seqs, heads, cap),
+        out_shape=[jax.ShapeDtypeStruct((seqs, heads, d, d), BF16)] + [packed_shape] * 3,
+        in_specs=[pl.BlockSpec(memory_space=pltpu.VMEM)] * 7,
+        out_specs=[pl.BlockSpec(memory_space=pltpu.VMEM)] + [pl.BlockSpec(memory_space=pl.ANY)] * 3,
+        scratch_shapes=[
+            vm((seqs // 2, 2, heads, d, d), BF16),
+            vm((total, rows), BF16),
+            vm((rows * HG, d), F32),
+            vm((rows, HG * d), BF16),
+            vm((3, total, HG * d), BF16),
+            dma((3,)),
+        ]
+        + [vm((share[k], 2, heads, d, d), BF16) for k in range(1, levels)]
         + [vm((seqs,) + facts.shape, F32), vm(((2 * levels + 1) * seqs, heads, d), F32)]
         + [dma((seqs - 1,)), dma((seqs - 1,))]
-        + [vm((share[k], heads, d, d), BF16) for k in range(levels)]
         + [vm((share[k], heads, d, d), BF16) for k in range(levels)]
         + [vm((heads, d, d), ZT), vm((heads, d, d), ZT)]
         + [dma((levels, chunks)), dma((levels, chunks))]
         + [dma((seqs - 1, chunks)), dma((seqs - 1, chunks))]
         + [dma((chunks,)), dma((chunks,))],
         compiler_params=pltpu.CompilerParams(
-            collective_id=call, has_side_effects=True, vmem_limit_bytes=60 * 1024 * 1024
+            collective_id=call, has_side_effects=True, vmem_limit_bytes=67043328
         ),
-    )(facts, rate, updates.reshape(seqs // 2, 2, heads, d, d))
+    )(facts, rate, flat.reshape(1, rows), key, value, query, kw)
 
 
 def finish_kernel(
@@ -453,23 +448,29 @@
         (doc == 0)[:, :, None], jnp.exp(-decay_rate[None, None, :] * since[None, :, None]), 0.0
     ).reshape(total, heads)
 
-    updates, key, value, query = updates_of(
-        flat, key_rows[0, 0], value_rows[0, 0], queries[0, 0], key_weight, loaders, cap
-    )
     passes = max(1, loaders // 8)
     width = heads // passes
-    states = [
-        scan_states(
-            facts,
-            rate[i * width : (i + 1) * width],
-            updates[:, i * width : (i + 1) * width],
-            levels,
-            shards,
-            i,
-        )
-        for i in range(passes)
+    results = []
+    for i in range(passes):
+        part = slice(i * width, (i + 1) * width)
+        results.append(
+            scan_states(
+                facts,
+                rate[part],
+                flat,
+                key_rows[0, 0, :, part],
+                value_rows[0, 0, :, part],
+                queries[0, 0, :, part],
+                key_weight[:, part],
+                levels,
+                shards,
+                cap,
+                i,
+            )
+        )
+    states, key, value, query = [
+        x[0] if passes == 1 else jnp.concatenate(x, axis=1) for x in zip(*results)
     ]
-    states = states[0] if passes == 1 else jnp.concatenate(states, axis=1)
     attended = finish(
         decay_rate, flat, query, key, value, states, doc, carry_weight, norm_gain, loaders, cap, heads, d
     )

time: 207 us -> 203 us (0.981)
  Pallas kernels: 196 us -> 189 us
    pallas_call x1 -> x0, Pallas kernels: 34 us -> none  [updates_of(): pl.pallas_call(functools.partial(update_kernel, seqs, cap), grid=(heads /...]
    pallas_call x1, Pallas kernels: 127 us -> 154 us  [scan_states(): pl.pallas_call(functools.partial(scan_kernel, levels, shards, seqs, heads...]
where the time goes in v1:
time: 203 us
  Pallas kernels  189 us (93%)
  other arithmetic  8.97 us (4%)
  local copies, waits for them, and re-layouts  4.29 us (2%)
    pallas_call x1, Pallas kernels, scan_states(): pl.pallas_call(functools.partial(scan_kernel, levels, shards, seqs, heads...  154 us
    pallas_call x1, Pallas kernels, finish(): pl.pallas_call(functools.partial(finish_kernel, heads, d), grid=(seqs,),...  34.8 us

profile of v1, /device:TPU:27, one launch (start us, length us, event | category | flops | bytes accessed | tf_op | source)
XLA Modules:
  0.0 202.5 jit_solution(11906459161836332144)
XLA Ops:
  0.0 0.8 convert_reduce_fusion.1
  0.8 0.7 neg.5
  1.5 1.0 convert_reduce_fusion
  2.5 0.7 bitcast_add_fusion.1
  3.2 1.3 bitcast_add_fusion.refs_2_
  4.4 0.7 multiply_add_fusion
  5.1 0.9 select_reduce_fusion
  6.0 0.1 reshape.211
  6.1 0.1 reduce_sum.53
  6.2 0.1 mul.88
  6.3 0.1 maximum_convert_fusion
  6.4 0.1 convert_element_type.42
  6.5 0.7 broadcast_in_dim.57.refs_0_
  7.1 1.3 broadcast_in_dim.86.refs_1_
  8.5 0.1 multiply_exponential_fusion
  8.6 0.2 multiply_reduce_fusion
  8.8 0.0 copy-start
  8.8 0.1 broadcast_compare_fusion
  8.9 0.1 eq.77
  9.0 0.1 and.15
  9.0 0.9 copy.17.flat_ref
  9.9 0.9 bitcast_select_fusion.cw_ref
  10.8 0.0 copy-done
  10.8 1.0 reshape.215.col_ref
  11.9 1.4 exponential_select_fusion.refs_6_
  13.3 154.4 %shard_map.73 = (bf16[8,32,128,128]{3,2,1,0:T(8,128)(2,1)}, bf16[768,4096]{1,0:T(8,128)(2,1)}, bf16[768,4096]{1,0:T(8,128)(2,1)}, bf16[768,4096]{1,0:T(8,128)(2,1)}) custom-call(f32[2,8,128]{2,1,0:T(8,128)} %broadcast_in_dim.57.refs_0_, f32[32,128]{1,0:T(8,128)} %broadcast_in_dim.86.refs_1_, s32[1,512]{1,0:T(1,128)} %bitcast_add_fusion.refs_2_, ...), custom_call_target="tpu_custom_call" | custom-call | tf_op jit(solution)/shard_map/pallas_call | solution.py:301
  167.8 34.8 %shard_map.74 = bf16[512,32,128]{2,1,0:T(8,128)(2,1)} custom-call(f32[32]{0:T(128)} %rate_ref.1, s32[512,1]{1,0:T(8,128)} %copy.17.flat_ref, bf16[768,4096]{1,0:T(8,128)(2,1)} %get-tuple-element.9.q_ref, bf16[768,4096]{1,0:T(8,128)(2,1)} %get-tuple-element.10.k_ref, bf16[768,4096]{1,0:T(8,128)(2,1)} %get-tuple-element.11.v_ref, ...), custom_call_target="tpu_custom_call" | custom-call | tf_op jit(solution)/shard_map/pallas_call | solution.py:378
  (4 shorter events, 0.0 us)
Async XLA Ops:
  8.8 2.0 %copy-start = (s32[8,96]{1,0:T(8,128)}, s32[8,96]{1,0:T(8,128)S(1)}, u32[]{:S(2)}) copy-start(s32[8,96]{1,0:T(8,128)S(1)} %multiply_reduce_fusion) | copy-start | bytes 9220
